TPU v7x, 512 devices: a whole 4x8x8 slice. The times are simulated.
512 devices in a mesh: gz: 32 (over z_hi, x, core), gy: 16 (over z_lo, y).
Axes of the slice: x: 4, y: 8, z: 8 (z_hi: 4, z_lo: 2; z = z_hi * 2 + z_lo), core: 2. Of those that a mesh axis runs over, the one named last changes fastest.
Arguments:
- filtered: bfloat16 [16, 256, 4096], P(None, 'gz', 'gy'), may hold values from -6 to 6
- angle_index: int32 [16], replicated, may hold values from 0 to 3599
- band_offset: int32 [16, 32], P(None, 'gz'), may hold values from 0 to 12, as said below
- band_length: int32 [16, 32], P(None, 'gz'), may hold values from 4 to 12
- foot_block: int32 [16, 64, 64], P(None, 'gy'), may hold values from 0 to 62, as said below
Outputs:
- denoised: float32 [64, 256, 4096], P('gy', 'gz')
Inputs may be any that keep to these rules, and one draw needn't show every extreme that they name: band_offset + band_length <= 16 for every projection and group. foot_block[p, y, b] is b plus a shift of -2 to 2 that depends only on p and y, clipped to the range.
All inputs are finite; a program needn't handle non-finite values.
Results may differ from a plain program's by a relative error of at most 0.0041.
Values may be sent and summed in bfloat16 or wider, within the bound.
A program may use at most 64 MiB of HBM per device.

v0:
```python
import math
import jax
import jax.numpy as jnp
from jax import lax
from jax.sharding import PartitionSpec as P

X = 4096
P_SIZE = 16
NANG = 3600
BLOCK = 64
ITERS = 2
step_length = 0.25
smooth_weight = 0.3
gradient_floor = 0.01
shift_reach = 8.0


def with_halo(cells, sides, width):
    for axis, dim in sides:
        count = lax.axis_size(axis)
        ends = count - 1
        head = lax.slice_in_dim(cells, 0, width, axis=dim)
        tail = lax.slice_in_dim(cells, cells.shape[dim] - width, cells.shape[dim], axis=dim)
        cells = jnp.concatenate(
            [
                lax.ppermute(tail, axis, [(i, (i + 1) % count) for i in range(ends)]),
                cells,
                lax.ppermute(head, axis, [((i + 1) % count, i) for i in range(ends)]),
            ],
            axis=dim,
        )
    return cells


def geometry(angle_value):
    radians = 2.0 * math.pi * angle_value.astype(jnp.float32) / NANG
    stretch = 0.5 + 0.5 * jnp.abs(jnp.cos(radians))
    spread = 1.0 + jnp.abs(jnp.sin(radians))
    return (radians, stretch, spread)


def footprint(radians, stretch, spread, row_global, rows_total, block_size):
    shifted = shift_reach * jnp.sin(radians + 2.0 * math.pi * row_global / rows_total)
    inside = jnp.arange(block_size).astype(jnp.float32) - 0.5 * (block_size - 1)
    centre = block_size + inside[None, :] * stretch + shifted[:, None]
    places = jnp.arange(2 * block_size).astype(jnp.float32) + 0.5
    weights = (
        jnp.maximum(0.0, 1.0 - jnp.abs(places[None, None, :] - centre[:, :, None]) / spread)
        / spread
    )
    return weights.astype(jnp.bfloat16)


def axial_table(offsets, lengths, depth_count):
    offset_real = offsets.astype(jnp.float32)[..., None]
    length_real = lengths.astype(jnp.float32)[..., None]
    depth_place = jnp.arange(depth_count).astype(jnp.float32) + 0.5
    centre = offset_real + depth_place * length_real / depth_count
    row_number = jnp.arange(2 * depth_count)
    row_place = row_number.astype(jnp.float32) + 0.5
    triangle = jnp.maximum(0.0, 1.0 - jnp.abs(row_place - centre[..., None]))
    inside = (row_number >= offsets[..., None, None]) & (
        row_number < (offsets + lengths)[..., None, None]
    )
    return jnp.where(inside, triangle, 0.0).astype(jnp.bfloat16)


def smooth_update(current, fidelity, row_first, depth_first, rows_total, depth_total):
    row_index = row_first + jnp.arange(current.shape[0])
    depth_index = depth_first + jnp.arange(current.shape[1])
    keep_rows = ((row_index >= 0) & (row_index < rows_total - 1)).astype(jnp.float32)[:, None, None]
    keep_depth = ((depth_index >= 0) & (depth_index < depth_total - 1)).astype(jnp.float32)[
        None, :, None
    ]
    forward_rows = (
        jnp.concatenate([current[1:] - current[:-1], jnp.zeros_like(current[:1])], 0) * keep_rows
    )
    forward_depth = (
        jnp.concatenate([current[:, 1:] - current[:, :-1], jnp.zeros_like(current[:, :1])], 1)
        * keep_depth
    )
    forward_width = jnp.concatenate(
        [current[:, :, 1:] - current[:, :, :-1], jnp.zeros_like(current[:, :, :1])], 2
    )
    magnitude = jnp.sqrt(
        forward_rows * forward_rows
        + forward_depth * forward_depth
        + forward_width * forward_width
        + gradient_floor
    )
    normal_rows = forward_rows / magnitude
    normal_depth = forward_depth / magnitude
    normal_width = forward_width / magnitude
    divergence = normal_rows - jnp.concatenate(
        [jnp.zeros_like(normal_rows[:1]), normal_rows[:-1]], 0
    )
    divergence = (
        divergence
        + normal_depth
        - jnp.concatenate([jnp.zeros_like(normal_depth[:, :1]), normal_depth[:, :-1]], 1)
    )
    divergence = (
        divergence
        + normal_width
        - jnp.concatenate([jnp.zeros_like(normal_width[:, :, :1]), normal_width[:, :, :-1]], 2)
    )
    return current + step_length * (smooth_weight * divergence - (current - fidelity))


def per_device(filtered, angle_index, band_offset, band_length, foot_block):
    depth_count = filtered.shape[1]
    row_count = foot_block.shape[1]
    extended_band = with_halo(filtered, (("gz", 1),), depth_count // 2)
    axial_weights = axial_table(band_offset[:, 0], band_length[:, 0], depth_count)
    summed_rows = jnp.einsum(
        "pzv,pvu->pzu",
        axial_weights,
        lax.all_gather(extended_band, "gy", axis=2, tiled=True),
        preferred_element_type=jnp.float32,
    )
    columns = summed_rows.astype(jnp.bfloat16)
    column_count = columns.shape[2]
    row_base = lax.axis_index("gy") * row_count
    depth_base = lax.axis_index("gz") * depth_count
    rows_total = lax.axis_size("gy") * row_count
    depth_total = lax.axis_size("gz") * depth_count
    row_global = (row_base + jnp.arange(row_count)).astype(jnp.float32)

    def one_projection(running, inputs):
        projected, angle_value, blocks = inputs
        radians, stretch, spread = geometry(angle_value)
        weights = footprint(radians, stretch, spread, row_global, rows_total, BLOCK)
        column_tiles = projected.reshape(depth_count, column_count // BLOCK, BLOCK)
        window = jnp.concatenate([column_tiles[:, blocks], column_tiles[:, blocks + 1]], axis=-1)
        product = jnp.einsum("yiu,zybu->yzbi", weights, window, preferred_element_type=jnp.float32)
        return (running + product.reshape(running.shape), None)

    initial = jnp.zeros((row_count, depth_count, X), jnp.float32)
    summed, _unused = lax.scan(one_projection, initial, (columns, angle_index, foot_block))
    backprojection = math.pi / P_SIZE * summed
    current = backprojection
    padded_fidelity = jnp.pad(backprojection, ((1, 1), (1, 1), (0, 0)))
    for turn_index in range(ITERS):
        extended = with_halo(current, (("gz", 1), ("gy", 0)), 1)
        updated = smooth_update(
            extended, padded_fidelity, row_base - 1, depth_base - 1, rows_total, depth_total
        )
        current = updated[1:-1, 1:-1]
    return current


def solution(mesh):
    return jax.shard_map(
        per_device,
        mesh=mesh,
        in_specs=(P(None, "gz", "gy"), P(), P(None, "gz"), P(None, "gz"), P(None, "gy", None)),
        out_specs=P("gy", "gz", None),
        check_vma=False,
    )
```

profile of v0, /device:TPU:191, one launch (start us, length us, event | category | flops | bytes accessed | tf_op | source)
XLA Modules:
  0.0 257.0 jit_solution(1076519616723766050)
XLA Ops:
  7.5 7.5 %collective-permute-start = (bf16[16,4,256]{2,1,0:T(4,128)(2,1)S(1)}, bf16[16,4,256]{2,1,0:T(4,128)(2,1)S(1)}, u32[]{:S(2)}, u32[]{:S(2)}) collective-permute-start(bf16[16,4,256]{2,1,0:T(4,128)(2,1)S(1)} %get-tuple-element.140), channel_id=1, source_target_pairs={{0,16},{16,32},{32,48},{48,64},{64,80},{80,96},{96,112},{112,128},... | collective-permute-start | bytes 98312 | tf_op jit(solution)/shard_map/ppermute | solution.py:26
  15.0 1.9 collective-permute-start.1
  16.9 7.5 %collective-permute-done.1 = bf16[16,4,256]{2,1,0:T(4,128)(2,1)S(1)} collective-permute-done((bf16[16,4,256]{2,1,0:T(4,128)(2,1)S(1)}, bf16[16,4,256]{2,1,0:T(4,128)(2,1)S(1)}, u32[]{:S(2)}, u32[]{:S(2)}) %collective-permute-start.1) | collective-permute-done | bytes 32800 | tf_op jit(solution)/shard_map/ppermute | solution.py:28
  24.4 1.6 pad_maximum_fusion.8
  28.2 60.6 %all-gather.2.cloned.1.call-done = bf16[16,16,4096]{2,1,0:T(8,128)(2,1)} async-done(((bf16[16,16,256]{2,1,0:T(8,128)(2,1)}), bf16[16,16,4096]{2,1,0:T(8,128)(2,1)}) %all-gather.2.cloned.1.call-update) | async-done | bytes 2097168 | tf_op jit(solution)/shard_map/all_gather | solution.py:118
  88.8 2.1 convolution_convert_fusion
  90.9 90.2 %while.13 = (s32[]{:T(128)}, f32[4,8,4096]{2,1,0:T(8,128)S(1)}, bf16[16,8,4096]{2,1,0:T(8,128)(2,1)S(1)}, s32[16,4,64]{2,1,0:T(4,128)}, s32[16]{0:T(128)S(1)}, /...) while((s32[]{:T(128)}, f32[4,8,4096]{2,1,0:T(8,128)S(1)}, ...), condition=%wide.region_1.2_spmd.clone, body=%wide.region_0.1_spmd.clone.sunk | while | flops 35099164 | bytes 6183707 | solution.py:139
  181.3 15.5 %collective-permute-start.2 = (f32[4,1,4096]{2,1,0:T(1,128)S(1)}, f32[4,1,4096]{2,1,0:T(1,128)S(1)}, u32[]{:S(2)}, u32[]{:S(2)}) collective-permute-start(f32[4,1,4096]{2,1,0:T(1,128)S(1)} %get-tuple-element.138), channel_id=1, source_target_pairs={{0,16},{16,32},{32,48},{48,64},{64,80},{80,96},{96,112},{112,128},... | collective-permute-start | bytes 196616 | tf_op jit(solution)/shard_map/ppermute | solution.py:26
  196.9 1.9 collective-permute-start.3
  198.8 8.6 %collective-permute-done.3 = f32[4,1,4096]{2,1,0:T(1,128)S(1)} collective-permute-done((f32[4,1,4096]{2,1,0:T(1,128)S(1)}, f32[4,1,4096]{2,1,0:T(1,128)S(1)}, u32[]{:S(2)}, u32[]{:S(2)}) %collective-permute-start.3) | collective-permute-done | bytes 65568 | tf_op jit(solution)/shard_map/ppermute | solution.py:28
  207.5 1.9 collective-permute-start.4
  209.4 3.4 %collective-permute-start.5 = (f32[1,10,4096]{2,1,0:T(8,128)S(1)}, f32[1,10,4096]{2,1,0:T(8,128)S(1)}, u32[]{:S(2)}, u32[]{:S(2)}) collective-permute-start(f32[1,10,4096]{2,1,0:T(8,128)S(1)} %get-tuple-element.137), channel_id=1, source_target_pairs={{1,0},{2,1},{3,2},{4,3},{5,4},{6,5},{7,6},{8,7},{9,8},{10,9},{11,1... | collective-permute-start | bytes 491528 | tf_op jit(solution)/shard_map/ppermute | solution.py:28
  212.8 1.8 collective-permute-done.4
  214.6 4.0 %collective-permute-done.5 = f32[1,10,4096]{2,1,0:T(8,128)S(1)} collective-permute-done((f32[1,10,4096]{2,1,0:T(8,128)S(1)}, f32[1,10,4096]{2,1,0:T(8,128)S(1)}, u32[]{:S(2)}, u32[]{:S(2)}) %collective-permute-start.5) | collective-permute-done | bytes 163872 | tf_op jit(solution)/shard_map/ppermute | solution.py:28
  221.0 1.2 multiply_add_fusion.1
  222.3 2.9 %collective-permute-start.6 = (f32[4,1,4096]{2,1,0:T(1,128)S(1)}, f32[4,1,4096]{2,1,0:T(1,128)S(1)}, u32[]{:S(2)}, u32[]{:S(2)}) collective-permute-start(f32[4,1,4096]{2,1,0:T(1,128)S(1)} %get-tuple-element.132), channel_id=1, source_target_pairs={{0,16},{16,32},{32,48},{48,64},{64,80},{80,96},{96,112},{112,128},... | collective-permute-start | bytes 196616 | tf_op jit(solution)/shard_map/ppermute | solution.py:26
  225.1 1.9 collective-permute-start.7
  227.1 7.8 %collective-permute-done.7 = f32[4,1,4096]{2,1,0:T(1,128)S(1)} collective-permute-done((f32[4,1,4096]{2,1,0:T(1,128)S(1)}, f32[4,1,4096]{2,1,0:T(1,128)S(1)}, u32[]{:S(2)}, u32[]{:S(2)}) %collective-permute-start.7) | collective-permute-done | bytes 65568 | tf_op jit(solution)/shard_map/ppermute | solution.py:28
  235.0 1.9 collective-permute-start.8
  237.0 3.4 %collective-permute-start.9 = (f32[1,10,4096]{2,1,0:T(8,128)S(1)}, f32[1,10,4096]{2,1,0:T(8,128)S(1)}, u32[]{:S(2)}, u32[]{:S(2)}) collective-permute-start(f32[1,10,4096]{2,1,0:T(8,128)S(1)} %get-tuple-element.135), channel_id=1, source_target_pairs={{1,0},{2,1},{3,2},{4,3},{5,4},{6,5},{7,6},{8,7},{9,8},{10,9},{11,1... | collective-permute-start | bytes 491528 | tf_op jit(solution)/shard_map/ppermute | solution.py:28
  240.3 1.8 collective-permute-done.8
  242.1 4.0 %collective-permute-done.9 = f32[1,10,4096]{2,1,0:T(8,128)S(1)} collective-permute-done((f32[1,10,4096]{2,1,0:T(8,128)S(1)}, f32[1,10,4096]{2,1,0:T(8,128)S(1)}, u32[]{:S(2)}, u32[]{:S(2)}) %collective-permute-start.9) | collective-permute-done | bytes 163872 | tf_op jit(solution)/shard_map/ppermute | solution.py:28
  247.3 1.1 fusion.20
  249.0 1.2 fusion.25
  (339 shorter events, 83.5 us)
Async XLA Ops:
  6.5 82.3 %all-gather.2.cloned.1.call-start = ((), (), s32[]{:S(2)}) async-start(), calls=%async_computation | async-start | bytes 2228224 | tf_op jit(solution)/shard_map/all_gather | solution.py:118
  7.5 9.4 %collective-permute-start = (bf16[16,4,256]{2,1,0:T(4,128)(2,1)S(1)}, bf16[16,4,256]{2,1,0:T(4,128)(2,1)S(1)}, u32[]{:S(2)}, u32[]{:S(2)}) collective-permute-start(bf16[16,4,256]{2,1,0:T(4,128)(2,1)S(1)} %get-tuple-element.140), channel_id=1, source_target_pairs={{0,16},{16,32},{32,48},{48,64},{64,80},{80,96},{96,112},{112,128},... | collective-permute-start | bytes 98312 | tf_op jit(solution)/shard_map/ppermute | solution.py:26
  15.0 9.5 %collective-permute-start.1 = (bf16[16,4,256]{2,1,0:T(4,128)(2,1)S(1)}, bf16[16,4,256]{2,1,0:T(4,128)(2,1)S(1)}, u32[]{:S(2)}, u32[]{:S(2)}) collective-permute-start(bf16[16,4,256]{2,1,0:T(4,128)(2,1)S(1)} %get-tuple-element.141), channel_id=1, source_target_pairs={{16,0},{32,16},{48,32},{64,48},{80,64},{96,80},{112,96},{128,112},... | collective-permute-start | bytes 98312 | tf_op jit(solution)/shard_map/ppermute | solution.py:28
  28.2 62.7 %copy-start = (s32[16]{0:T(128)S(1)}, s32[16]{0:T(128)}, u32[]{:S(2)}) copy-start(s32[16]{0:T(128)} %param.8) | copy-start | bytes 196
  181.3 17.5 %collective-permute-start.2 = (f32[4,1,4096]{2,1,0:T(1,128)S(1)}, f32[4,1,4096]{2,1,0:T(1,128)S(1)}, u32[]{:S(2)}, u32[]{:S(2)}) collective-permute-start(f32[4,1,4096]{2,1,0:T(1,128)S(1)} %get-tuple-element.138), channel_id=1, source_target_pairs={{0,16},{16,32},{32,48},{48,64},{64,80},{80,96},{96,112},{112,128},... | collective-permute-start | bytes 196616 | tf_op jit(solution)/shard_map/ppermute | solution.py:26
  196.9 10.5 %collective-permute-start.3 = (f32[4,1,4096]{2,1,0:T(1,128)S(1)}, f32[4,1,4096]{2,1,0:T(1,128)S(1)}, u32[]{:S(2)}, u32[]{:S(2)}) collective-permute-start(f32[4,1,4096]{2,1,0:T(1,128)S(1)} %get-tuple-element.139), channel_id=1, source_target_pairs={{16,0},{32,16},{48,32},{64,48},{80,64},{96,80},{112,96},{128,112},... | collective-permute-start | bytes 196616 | tf_op jit(solution)/shard_map/ppermute | solution.py:28
  207.5 7.1 %collective-permute-start.4 = (f32[1,10,4096]{2,1,0:T(8,128)S(1)}, f32[1,10,4096]{2,1,0:T(8,128)S(1)}, u32[]{:S(2)}, u32[]{:S(2)}) collective-permute-start(f32[1,10,4096]{2,1,0:T(8,128)S(1)} %get-tuple-element.136), channel_id=1, source_target_pairs={{0,1},{1,2},{2,3},{3,4},{4,5},{5,6},{6,7},{7,8},{8,9},{9,10},{10,1... | collective-permute-start | bytes 491528 | tf_op jit(solution)/shard_map/ppermute | solution.py:26
  209.4 9.2 %collective-permute-start.5 = (f32[1,10,4096]{2,1,0:T(8,128)S(1)}, f32[1,10,4096]{2,1,0:T(8,128)S(1)}, u32[]{:S(2)}, u32[]{:S(2)}) collective-permute-start(f32[1,10,4096]{2,1,0:T(8,128)S(1)} %get-tuple-element.137), channel_id=1, source_target_pairs={{1,0},{2,1},{3,2},{4,3},{5,4},{6,5},{7,6},{8,7},{9,8},{10,9},{11,1... | collective-permute-start | bytes 491528 | tf_op jit(solution)/shard_map/ppermute | solution.py:28
  222.3 4.9 %collective-permute-start.6 = (f32[4,1,4096]{2,1,0:T(1,128)S(1)}, f32[4,1,4096]{2,1,0:T(1,128)S(1)}, u32[]{:S(2)}, u32[]{:S(2)}) collective-permute-start(f32[4,1,4096]{2,1,0:T(1,128)S(1)} %get-tuple-element.132), channel_id=1, source_target_pairs={{0,16},{16,32},{32,48},{48,64},{64,80},{80,96},{96,112},{112,128},... | collective-permute-start | bytes 196616 | tf_op jit(solution)/shard_map/ppermute | solution.py:26
  225.1 9.8 %collective-permute-start.7 = (f32[4,1,4096]{2,1,0:T(1,128)S(1)}, f32[4,1,4096]{2,1,0:T(1,128)S(1)}, u32[]{:S(2)}, u32[]{:S(2)}) collective-permute-start(f32[4,1,4096]{2,1,0:T(1,128)S(1)} %get-tuple-element.133), channel_id=1, source_target_pairs={{16,0},{32,16},{48,32},{64,48},{80,64},{96,80},{112,96},{128,112},... | collective-permute-start | bytes 196616 | tf_op jit(solution)/shard_map/ppermute | solution.py:28
  235.0 7.1 %collective-permute-start.8 = (f32[1,10,4096]{2,1,0:T(8,128)S(1)}, f32[1,10,4096]{2,1,0:T(8,128)S(1)}, u32[]{:S(2)}, u32[]{:S(2)}) collective-permute-start(f32[1,10,4096]{2,1,0:T(8,128)S(1)} %get-tuple-element.134), channel_id=1, source_target_pairs={{0,1},{1,2},{2,3},{3,4},{4,5},{5,6},{6,7},{7,8},{8,9},{9,10},{10,1... | collective-permute-start | bytes 491528 | tf_op jit(solution)/shard_map/ppermute | solution.py:26
  237.0 9.2 %collective-permute-start.9 = (f32[1,10,4096]{2,1,0:T(8,128)S(1)}, f32[1,10,4096]{2,1,0:T(8,128)S(1)}, u32[]{:S(2)}, u32[]{:S(2)}) collective-permute-start(f32[1,10,4096]{2,1,0:T(8,128)S(1)} %get-tuple-element.135), channel_id=1, source_target_pairs={{1,0},{2,1},{3,2},{4,3},{5,4},{6,5},{7,6},{8,7},{9,8},{10,9},{11,1... | collective-permute-start | bytes 491528 | tf_op jit(solution)/shard_map/ppermute | solution.py:28
Sparse Core Ops, SparseCore 0:
  26.1 62.6 all-gather.1
where the time goes:
time: 258 us; the launch traced here: 257 us
  waiting for transfers between devices  96.2 us (37%)
  local copies, waits for them, and re-layouts  54.1 us (21%)
  starting transfers between devices  42.2 us (16%)
  other arithmetic  26.9 us (10%)
  loops' own time  14.3 us (6%)
  between operations  13.7 us (5%)
  matrix products  9.54 us (4%)
    all_gather x1, waiting for transfers between devices, per_device(): lax.all_gather(extended_band, 'gy', axis=2, tiled=True)  60.6 us
    ppermute x5, waiting for transfers between devices, with_halo(): lax.ppermute(head, axis, [((i + 1) % count, i) for i in range(ends)])  32 us
    ppermute x5, starting transfers between devices, with_halo(): lax.ppermute(tail, axis, [(i, (i + 1) % count) for i in range(ends)])  29.7 us
    gather x32, local copies, waits for them, and re-layouts, one_projection(): column_tiles[:, blocks + 1]  17.4 us
    another operation x1, loops' own time, per_device(): lax.scan(one_projection, initial, (columns, angle_index, foot_block))  14.3 us
    gather x16, local copies, waits for them, and re-layouts, one_projection(): column_tiles[:, blocks]  13.1 us
    ppermute x5, starting transfers between devices, with_halo(): lax.ppermute(head, axis, [((i + 1) % count, i) for i in range(ends)])  12.5 us
    select_n x16, other arithmetic, one_projection(): column_tiles[:, blocks]  11 us
  transfers between devices with their start and end apart: 11, of which 8 were waited for; matrix products, arithmetic and copies ran while one was open for 1% of the time, Pallas kernels for 0%

commit v1 on v0

--- a/solution.py
+++ b/solution.py
@@ -115,7 +115,9 @@
     summed_rows = jnp.einsum(
         "pzv,pvu->pzu",
         axial_weights,
-        lax.all_gather(extended_band, "gy", axis=2, tiled=True),
+        jnp.concatenate(
+            lax.all_to_all(jnp.stack([extended_band] * lax.axis_size("gy")), "gy", 0, 0), axis=2
+        ),
         preferred_element_type=jnp.float32,
     )
     columns = summed_rows.astype(jnp.bfloat16)

time: 258 us -> 227 us (0.88)
  waiting for transfers between devices: 96.2 us -> 79.1 us
  between operations: 13.7 us -> 0.35 us
  local copies, waits for them, and re-layouts: 54.1 us -> 58.9 us
  other arithmetic: 26.9 us -> 24.3 us
    all_gather x1 -> x0, waiting for transfers between devices: 60.6 us -> none  [per_device(): lax.all_gather(extended_band, 'gy', axis=2, tiled=True)]
    all_to_all x0 -> x1, waiting for transfers between devices: none -> 42.1 us  [per_device(): lax.all_to_all(jnp.stack([extended_band] * lax.axis_size('gy')), 'gy', 0, 0)]
    ppermute x5, starting transfers between devices: 29.7 us -> 21.8 us  [with_halo(): lax.ppermute(tail, axis, [(i, (i + 1) % count) for i in range(ends)])]
    all_to_all x0 -> x1, starting transfers between devices: none -> 7.41 us  [per_device(): lax.all_to_all(jnp.stack([extended_band] * lax.axis_size('gy')), 'gy', 0, 0)]
  transfers between devices with their start and end apart: 11 -> 11, of which waited for: 8 -> 8; matrix products, arithmetic and copies ran while one was open for 1% -> 0% of each run, Pallas kernels for 0% -> 0%
where the time goes in v1:
time: 227 us; the launch traced here: 226 us
  waiting for transfers between devices  79.1 us (35%)
  local copies, waits for them, and re-layouts  58.9 us (26%)
  starting transfers between devices  40.2 us (18%)
  other arithmetic  24.3 us (11%)
  loops' own time  15 us (7%)
  matrix products  7.94 us (3%)
    all_to_all x1, waiting for transfers between devices, per_device(): lax.all_to_all(jnp.stack([extended_band] * lax.axis_size('gy')), 'gy', 0, 0)  42.1 us
    ppermute x5, waiting for transfers between devices, with_halo(): lax.ppermute(head, axis, [((i + 1) % count, i) for i in range(ends)])  33.6 us
    ppermute x5, starting transfers between devices, with_halo(): lax.ppermute(tail, axis, [(i, (i + 1) % count) for i in range(ends)])  21.8 us
    gather x32, local copies, waits for them, and re-layouts, one_projection(): column_tiles[:, blocks + 1]  17.4 us
    another operation x1, loops' own time, per_device(): lax.scan(one_projection, initial, (columns, angle_index, foot_block))  15 us
    gather x16, local copies, waits for them, and re-layouts, one_projection(): column_tiles[:, blocks]  13.1 us
    ppermute x5, starting transfers between devices, with_halo(): lax.ppermute(head, axis, [((i + 1) % count, i) for i in range(ends)])  11 us
    select_n x16, other arithmetic, one_projection(): column_tiles[:, blocks]  11 us
  transfers between devices with their start and end apart: 11, of which 8 were waited for; matrix products, arithmetic and copies ran while one was open for 0% of the time, Pallas kernels for 0%

profile of v1, /device:TPU:191, one launch (start us, length us, event | category | flops | bytes accessed | tf_op | source)
XLA Modules:
  0.0 225.8 jit_solution(17027110156071805583)
XLA Ops:
  0.9 7.5 %collective-permute-start = (bf16[16,4,256]{2,1,0:T(4,128)(2,1)S(1)}, bf16[16,4,256]{2,1,0:T(4,128)(2,1)S(1)}, u32[]{:S(2)}, u32[]{:S(2)}) collective-permute-start(bf16[16,4,256]{2,1,0:T(4,128)(2,1)S(1)} %get-tuple-element.140), channel_id=1, source_target_pairs={{0,16},{16,32},{32,48},{48,64},{64,80},{80,96},{96,112},{112,128},... | collective-permute-start | bytes 98312 | tf_op jit(solution)/shard_map/ppermute | solution.py:26
  8.4 1.9 collective-permute-start.1
  10.4 7.5 %collective-permute-done.1 = bf16[16,4,256]{2,1,0:T(4,128)(2,1)S(1)} collective-permute-done((bf16[16,4,256]{2,1,0:T(4,128)(2,1)S(1)}, bf16[16,4,256]{2,1,0:T(4,128)(2,1)S(1)}, u32[]{:S(2)}, u32[]{:S(2)}) %collective-permute-start.1) | collective-permute-done | bytes 32800 | tf_op jit(solution)/shard_map/ppermute | solution.py:28
  18.8 1.5 stack.2
  20.3 7.4 %all-to-all-start = ((bf16[16,16,16,256]{3,2,1,0:T(8,128)(2,1)}), bf16[16,16,16,256]{3,2,1,0:T(8,128)(2,1)}, u32[]{:S(2)}, u32[]{:S(2)}) async-start(bf16[16,16,16,256]{3,2,1,0:T(8,128)(2,1)} %stack.2), calls=%async_computation | async-start | bytes 4194304 | tf_op jit(solution)/shard_map/all_to_all | solution.py:119
  28.0 42.1 %all-to-all-done = bf16[16,16,16,256]{3,2,1,0:T(8,128)(2,1)} async-done(((bf16[16,16,16,256]{3,2,1,0:T(8,128)(2,1)}), bf16[16,16,16,256]{3,2,1,0:T(8,128)(2,1)}, u32[]{:S(2)}, u32[]{:S(2)}) %all-to-all-start) | async-done | bytes 2097184 | tf_op jit(solution)/shard_map/all_to_all | solution.py:119
  70.1 1.8 copy.28
  72.6 92.2 %while.13 = (s32[]{:T(128)}, f32[4,8,4096]{2,1,0:T(8,128)S(1)}, bf16[16,8,4096]{2,1,0:T(8,128)(2,1)S(1)}, s32[16,4,64]{2,1,0:T(4,128)}, s32[16]{0:T(128)S(1)}, /...) while((s32[]{:T(128)}, f32[4,8,4096]{2,1,0:T(8,128)S(1)}, ...), condition=%wide.region_1.2_spmd.clone, body=%wide.region_0.1_spmd.clone.sunk | while | flops 35099164 | bytes 6183707 | solution.py:141
  164.9 5.4 %collective-permute-start.2 = (f32[4,1,4096]{2,1,0:T(1,128)S(1)}, f32[4,1,4096]{2,1,0:T(1,128)S(1)}, u32[]{:S(2)}, u32[]{:S(2)}) collective-permute-start(f32[4,1,4096]{2,1,0:T(1,128)S(1)} %get-tuple-element.138), channel_id=1, source_target_pairs={{0,16},{16,32},{32,48},{48,64},{64,80},{80,96},{96,112},{112,128},... | collective-permute-start | bytes 196616 | tf_op jit(solution)/shard_map/ppermute | solution.py:26
  170.4 1.9 collective-permute-start.3
  172.3 7.9 %collective-permute-done.3 = f32[4,1,4096]{2,1,0:T(1,128)S(1)} collective-permute-done((f32[4,1,4096]{2,1,0:T(1,128)S(1)}, f32[4,1,4096]{2,1,0:T(1,128)S(1)}, u32[]{:S(2)}, u32[]{:S(2)}) %collective-permute-start.3) | collective-permute-done | bytes 65568 | tf_op jit(solution)/shard_map/ppermute | solution.py:28
  180.2 3.7 %collective-permute-start.4 = (f32[1,10,4096]{2,1,0:T(8,128)S(1)}, f32[1,10,4096]{2,1,0:T(8,128)S(1)}, u32[]{:S(2)}, u32[]{:S(2)}) collective-permute-start(f32[1,10,4096]{2,1,0:T(8,128)S(1)} %get-tuple-element.136), channel_id=1, source_target_pairs={{0,1},{1,2},{2,3},{3,4},{4,5},{5,6},{6,7},{7,8},{8,9},{9,10},{10,1... | collective-permute-start | bytes 491528 | tf_op jit(solution)/shard_map/ppermute | solution.py:26
  184.0 1.9 collective-permute-start.5
  185.9 1.6 collective-permute-done.4
  187.5 5.7 %collective-permute-done.5 = f32[1,10,4096]{2,1,0:T(8,128)S(1)} collective-permute-done((f32[1,10,4096]{2,1,0:T(8,128)S(1)}, f32[1,10,4096]{2,1,0:T(8,128)S(1)}, u32[]{:S(2)}, u32[]{:S(2)}) %collective-permute-start.5) | collective-permute-done | bytes 163872 | tf_op jit(solution)/shard_map/ppermute | solution.py:28
  195.5 1.2 multiply_add_fusion.1
  196.8 3.2 %collective-permute-start.6 = (f32[4,1,4096]{2,1,0:T(1,128)S(1)}, f32[4,1,4096]{2,1,0:T(1,128)S(1)}, u32[]{:S(2)}, u32[]{:S(2)}) collective-permute-start(f32[4,1,4096]{2,1,0:T(1,128)S(1)} %get-tuple-element.132), channel_id=1, source_target_pairs={{0,16},{16,32},{32,48},{48,64},{64,80},{80,96},{96,112},{112,128},... | collective-permute-start | bytes 196616 | tf_op jit(solution)/shard_map/ppermute | solution.py:26
  200.0 1.9 collective-permute-start.7
  202.1 8.5 %collective-permute-done.7 = f32[4,1,4096]{2,1,0:T(1,128)S(1)} collective-permute-done((f32[4,1,4096]{2,1,0:T(1,128)S(1)}, f32[4,1,4096]{2,1,0:T(1,128)S(1)}, u32[]{:S(2)}, u32[]{:S(2)}) %collective-permute-start.7) | collective-permute-done | bytes 65568 | tf_op jit(solution)/shard_map/ppermute | solution.py:28
  210.7 1.9 collective-permute-start.8
  212.6 3.4 %collective-permute-start.9 = (f32[1,10,4096]{2,1,0:T(8,128)S(1)}, f32[1,10,4096]{2,1,0:T(8,128)S(1)}, u32[]{:S(2)}, u32[]{:S(2)}) collective-permute-start(f32[1,10,4096]{2,1,0:T(8,128)S(1)} %get-tuple-element.135), channel_id=1, source_target_pairs={{1,0},{2,1},{3,2},{4,3},{5,4},{6,5},{7,6},{8,7},{9,8},{10,9},{11,1... | collective-permute-start | bytes 491528 | tf_op jit(solution)/shard_map/ppermute | solution.py:28
  216.0 1.8 collective-permute-done.8
  217.8 4.0 %collective-permute-done.9 = f32[1,10,4096]{2,1,0:T(8,128)S(1)} collective-permute-done((f32[1,10,4096]{2,1,0:T(8,128)S(1)}, f32[1,10,4096]{2,1,0:T(8,128)S(1)}, u32[]{:S(2)}, u32[]{:S(2)}) %collective-permute-start.9) | collective-permute-done | bytes 163872 | tf_op jit(solution)/shard_map/ppermute | solution.py:28
  224.6 1.2 fusion.25
  (344 shorter events, 85.4 us)
Async XLA Ops:
  0.9 9.4 %collective-permute-start = (bf16[16,4,256]{2,1,0:T(4,128)(2,1)S(1)}, bf16[16,4,256]{2,1,0:T(4,128)(2,1)S(1)}, u32[]{:S(2)}, u32[]{:S(2)}) collective-permute-start(bf16[16,4,256]{2,1,0:T(4,128)(2,1)S(1)} %get-tuple-element.140), channel_id=1, source_target_pairs={{0,16},{16,32},{32,48},{48,64},{64,80},{80,96},{96,112},{112,128},... | collective-permute-start | bytes 98312 | tf_op jit(solution)/shard_map/ppermute | solution.py:26
  8.4 9.5 %collective-permute-start.1 = (bf16[16,4,256]{2,1,0:T(4,128)(2,1)S(1)}, bf16[16,4,256]{2,1,0:T(4,128)(2,1)S(1)}, u32[]{:S(2)}, u32[]{:S(2)}) collective-permute-start(bf16[16,4,256]{2,1,0:T(4,128)(2,1)S(1)} %get-tuple-element.141), channel_id=1, source_target_pairs={{16,0},{32,16},{48,32},{64,48},{80,64},{96,80},{112,96},{128,112},... | collective-permute-start | bytes 98312 | tf_op jit(solution)/shard_map/ppermute | solution.py:28
  20.3 7.5 %copy-start = (s32[16,1]{0,1:T(1,128)S(1)}, s32[16,1]{0,1:T(1,128)}, u32[]{:S(2)}) copy-start(s32[16,1]{0,1:T(1,128)} %param.9) | copy-start | bytes 196
  20.3 7.5 %copy-start.1 = (s32[16,1]{0,1:T(1,128)S(1)}, s32[16,1]{0,1:T(1,128)}, u32[]{:S(2)}) copy-start(s32[16,1]{0,1:T(1,128)} %param.10) | copy-start | bytes 196
  20.3 49.7 %all-to-all-start = ((bf16[16,16,16,256]{3,2,1,0:T(8,128)(2,1)}), bf16[16,16,16,256]{3,2,1,0:T(8,128)(2,1)}, u32[]{:S(2)}, u32[]{:S(2)}) async-start(bf16[16,16,16,256]{3,2,1,0:T(8,128)(2,1)} %stack.2), calls=%async_computation | async-start | bytes 4194304 | tf_op jit(solution)/shard_map/all_to_all | solution.py:119
  71.9 0.7 copy-start.2
  164.9 7.4 %collective-permute-start.2 = (f32[4,1,4096]{2,1,0:T(1,128)S(1)}, f32[4,1,4096]{2,1,0:T(1,128)S(1)}, u32[]{:S(2)}, u32[]{:S(2)}) collective-permute-start(f32[4,1,4096]{2,1,0:T(1,128)S(1)} %get-tuple-element.138), channel_id=1, source_target_pairs={{0,16},{16,32},{32,48},{48,64},{64,80},{80,96},{96,112},{112,128},... | collective-permute-start | bytes 196616 | tf_op jit(solution)/shard_map/ppermute | solution.py:26
  170.4 9.8 %collective-permute-start.3 = (f32[4,1,4096]{2,1,0:T(1,128)S(1)}, f32[4,1,4096]{2,1,0:T(1,128)S(1)}, u32[]{:S(2)}, u32[]{:S(2)}) collective-permute-start(f32[4,1,4096]{2,1,0:T(1,128)S(1)} %get-tuple-element.139), channel_id=1, source_target_pairs={{16,0},{32,16},{48,32},{64,48},{80,64},{96,80},{112,96},{128,112},... | collective-permute-start | bytes 196616 | tf_op jit(solution)/shard_map/ppermute | solution.py:28
  180.2 7.3 %collective-permute-start.4 = (f32[1,10,4096]{2,1,0:T(8,128)S(1)}, f32[1,10,4096]{2,1,0:T(8,128)S(1)}, u32[]{:S(2)}, u32[]{:S(2)}) collective-permute-start(f32[1,10,4096]{2,1,0:T(8,128)S(1)} %get-tuple-element.136), channel_id=1, source_target_pairs={{0,1},{1,2},{2,3},{3,4},{4,5},{5,6},{6,7},{7,8},{8,9},{9,10},{10,1... | collective-permute-start | bytes 491528 | tf_op jit(solution)/shard_map/ppermute | solution.py:26
  184.0 9.2 %collective-permute-start.5 = (f32[1,10,4096]{2,1,0:T(8,128)S(1)}, f32[1,10,4096]{2,1,0:T(8,128)S(1)}, u32[]{:S(2)}, u32[]{:S(2)}) collective-permute-start(f32[1,10,4096]{2,1,0:T(8,128)S(1)} %get-tuple-element.137), channel_id=1, source_target_pairs={{1,0},{2,1},{3,2},{4,3},{5,4},{6,5},{7,6},{8,7},{9,8},{10,9},{11,1... | collective-permute-start | bytes 491528 | tf_op jit(solution)/shard_map/ppermute | solution.py:28
  196.8 5.2 %collective-permute-start.6 = (f32[4,1,4096]{2,1,0:T(1,128)S(1)}, f32[4,1,4096]{2,1,0:T(1,128)S(1)}, u32[]{:S(2)}, u32[]{:S(2)}) collective-permute-start(f32[4,1,4096]{2,1,0:T(1,128)S(1)} %get-tuple-element.132), channel_id=1, source_target_pairs={{0,16},{16,32},{32,48},{48,64},{64,80},{80,96},{96,112},{112,128},... | collective-permute-start | bytes 196616 | tf_op jit(solution)/shard_map/ppermute | solution.py:26
  200.0 10.5 %collective-permute-start.7 = (f32[4,1,4096]{2,1,0:T(1,128)S(1)}, f32[4,1,4096]{2,1,0:T(1,128)S(1)}, u32[]{:S(2)}, u32[]{:S(2)}) collective-permute-start(f32[4,1,4096]{2,1,0:T(1,128)S(1)} %get-tuple-element.133), channel_id=1, source_target_pairs={{16,0},{32,16},{48,32},{64,48},{80,64},{96,80},{112,96},{128,112},... | collective-permute-start | bytes 196616 | tf_op jit(solution)/shard_map/ppermute | solution.py:28
  210.7 7.1 %collective-permute-start.8 = (f32[1,10,4096]{2,1,0:T(8,128)S(1)}, f32[1,10,4096]{2,1,0:T(8,128)S(1)}, u32[]{:S(2)}, u32[]{:S(2)}) collective-permute-start(f32[1,10,4096]{2,1,0:T(8,128)S(1)} %get-tuple-element.134), channel_id=1, source_target_pairs={{0,1},{1,2},{2,3},{3,4},{4,5},{5,6},{6,7},{7,8},{8,9},{9,10},{10,1... | collective-permute-start | bytes 491528 | tf_op jit(solution)/shard_map/ppermute | solution.py:26
  212.6 9.2 %collective-permute-start.9 = (f32[1,10,4096]{2,1,0:T(8,128)S(1)}, f32[1,10,4096]{2,1,0:T(8,128)S(1)}, u32[]{:S(2)}, u32[]{:S(2)}) collective-permute-start(f32[1,10,4096]{2,1,0:T(8,128)S(1)} %get-tuple-element.135), channel_id=1, source_target_pairs={{1,0},{2,1},{3,2},{4,3},{5,4},{6,5},{7,6},{8,7},{9,8},{10,9},{11,1... | collective-permute-start | bytes 491528 | tf_op jit(solution)/shard_map/ppermute | solution.py:28
